TPU v7x, 32 devices: a whole 2x2x4 slice. The times are simulated.
32 devices in a mesh: blk: 16 (over z, y, core), uly: 2 (over x).
Axes of the slice: x: 2, y: 2, z: 4, core: 2. Of those that a mesh axis runs over, the one named last changes fastest.
Arguments:
- tokens: bfloat16 [4096, 5120], P(('blk', 'uly')), may hold values from -6 to 6
- query_base: bfloat16 [4096, 5120], P(('blk', 'uly')), may hold values from -9 to 9
- key_base: bfloat16 [4096, 5120], P(('blk', 'uly')), may hold values from -9 to 9
- value_base: bfloat16 [4096, 5120], P(('blk', 'uly')), may hold values from -6 to 6
- out_grad: bfloat16 [4096, 5120], P(('blk', 'uly')), may hold values from -0.059814453 to 0.059814453
- down_q: bfloat16 [5120, 64], replicated, may hold values from -0.078125 to 0.078125
- up_q: bfloat16 [64, 5120], replicated, may hold values from -0.75 to 0.75
- down_v: bfloat16 [5120, 64], replicated, may hold values from -0.078125 to 0.078125
- up_v: bfloat16 [64, 5120], replicated, may hold values from -0.75 to 0.75
Outputs:
- attended: bfloat16 [4096, 5120], P(('blk', 'uly'))
- grad_down_q: bfloat16 [5120, 64], replicated
- grad_up_q: bfloat16 [64, 5120], P(None, 'uly')
- grad_down_v: bfloat16 [5120, 64], replicated
- grad_up_v: bfloat16 [64, 5120], P(None, 'uly')
All inputs are finite; a program needn't handle non-finite values.
Results may differ from a plain program's by a relative error of at most 0.025.
Values may be sent and summed in bfloat16 or wider, within the bound.
A program may use at most 128 MiB of HBM per device.

v0:
```python
import jax
import jax.numpy as jnp
from jax import lax
from jax.sharding import PartitionSpec as P

HEAD = 128


def passed_along(block, axis, distance):
    devices = range(lax.axis_size(axis))
    route = [(i - distance, i) for i in devices if i - distance in devices]
    return lax.ppermute(block, axis, route)


def inner(left, right):
    return lax.dot_general(
        left, right, (((0,), (0,)), ((), ())), preferred_element_type=jnp.float32
    )


def head_pass(query, keys, values, upstream, usable, scale):
    scores = jnp.dot(query, keys.T, preferred_element_type=jnp.float32) * scale
    scores = jnp.where(usable[None, :], scores, -jnp.inf)
    top = jnp.max(scores, axis=1, keepdims=True)
    total = jnp.sum(jnp.exp(scores - top), axis=1, keepdims=True)
    probs = jnp.exp(scores - top - jnp.log(total)).astype(jnp.bfloat16)
    attended = jnp.dot(probs, values, preferred_element_type=jnp.float32).astype(jnp.bfloat16)
    delta = jnp.sum(
        upstream.astype(jnp.float32) * attended.astype(jnp.float32), axis=1, keepdims=True
    )
    prob_grad = jnp.dot(upstream, values.T, preferred_element_type=jnp.float32)
    score_grad = (probs.astype(jnp.float32) * (prob_grad - delta)).astype(jnp.bfloat16)
    query_grad = (jnp.dot(score_grad, keys, preferred_element_type=jnp.float32) * scale).astype(
        jnp.bfloat16
    )
    value_terms = jnp.dot(probs.T, upstream, preferred_element_type=jnp.float32)
    return (attended, query_grad, value_terms)


def per_device(tokens, query_base, key_base, value_base, out_grad, down_q, up_q, down_v, up_v):
    low_q = jnp.dot(tokens, down_q, preferred_element_type=jnp.float32).astype(jnp.bfloat16)
    low_v = jnp.dot(tokens, down_v, preferred_element_type=jnp.float32).astype(jnp.bfloat16)
    query = (
        query_base.astype(jnp.float32) + jnp.dot(low_q, up_q, preferred_element_type=jnp.float32)
    ).astype(jnp.bfloat16)
    value = (
        value_base.astype(jnp.float32) + jnp.dot(low_v, up_v, preferred_element_type=jnp.float32)
    ).astype(jnp.bfloat16)
    query_h, keys_h, values_h, upstream_h = (
        lax.all_to_all(query, "uly", split_axis=1, concat_axis=0, tiled=True),
        lax.all_to_all(key_base, "uly", split_axis=1, concat_axis=0, tiled=True),
        lax.all_to_all(value, "uly", split_axis=1, concat_axis=0, tiled=True),
        lax.all_to_all(out_grad, "uly", split_axis=1, concat_axis=0, tiled=True),
    )
    rows = query_h.shape[0]
    width = query_h.shape[1]
    heads_here = width // HEAD
    scale = HEAD ** (-0.5)
    earlier = passed_along(jnp.stack([keys_h, values_h]), "blk", 1)
    keys_all = jnp.concatenate([earlier[0], keys_h], 0)
    values_all = jnp.concatenate([earlier[1], values_h], 0)
    column = jnp.arange(2 * rows)
    usable = jnp.logical_or(column >= rows, lax.axis_index("blk") > 0)

    def per_head(index, carry):
        attended, query_grad, own_terms, prior_terms = carry
        start = index * HEAD
        result = head_pass(
            lax.dynamic_slice_in_dim(query_h, start, HEAD, 1),
            lax.dynamic_slice_in_dim(keys_all, start, HEAD, 1),
            lax.dynamic_slice_in_dim(values_all, start, HEAD, 1),
            lax.dynamic_slice_in_dim(upstream_h, start, HEAD, 1),
            usable,
            scale,
        )
        attended = lax.dynamic_update_slice_in_dim(attended, result[0], start, 1)
        query_grad = lax.dynamic_update_slice_in_dim(query_grad, result[1], start, 1)
        prior_terms = lax.dynamic_update_slice_in_dim(prior_terms, result[2][:rows], start, 1)
        own_terms = lax.dynamic_update_slice_in_dim(own_terms, result[2][rows:], start, 1)
        return (attended, query_grad, own_terms, prior_terms)

    empty_half = jnp.zeros((rows, width), jnp.bfloat16)
    empty_full = jnp.zeros((rows, width), jnp.float32)
    attended_h, query_grad_h, own_terms, prior_terms = lax.fori_loop(
        0, heads_here, per_head, (empty_half, empty_half, empty_full, empty_full)
    )
    returned = passed_along(prior_terms, "blk", -1)
    value_grad_h = (own_terms + returned).astype(jnp.bfloat16)
    rank = down_q.shape[1]
    first_col = lax.axis_index("uly") * width
    attended = lax.all_to_all(attended_h, "uly", split_axis=0, concat_axis=1, tiled=True)
    block_lows = lax.all_gather(jnp.concatenate([low_q, low_v], 1), "uly", axis=0, tiled=True)
    cols_q = lax.dynamic_slice_in_dim(up_q, first_col, width, 1)
    cols_v = lax.dynamic_slice_in_dim(up_v, first_col, width, 1)
    partial_rank = jnp.concatenate(
        [
            jnp.dot(query_grad_h, cols_q.T, preferred_element_type=jnp.float32),
            jnp.dot(value_grad_h, cols_v.T, preferred_element_type=jnp.float32),
        ],
        1,
    )
    lowrank = lax.psum_scatter(partial_rank, "uly", scatter_dimension=0, tiled=True).astype(
        jnp.bfloat16
    )
    down_total = lax.psum(inner(tokens, lowrank), ("blk", "uly"))
    up_q_terms = inner(block_lows[:, :rank], query_grad_h)
    up_v_terms = inner(block_lows[:, rank:], value_grad_h)
    up_q_part, up_v_part = (
        lax.psum(up_q_terms.astype(jnp.bfloat16), "blk").astype(jnp.float32),
        lax.psum(up_v_terms.astype(jnp.bfloat16), "blk").astype(jnp.float32),
    )
    return (
        attended,
        down_total[:, :rank].astype(jnp.bfloat16),
        up_q_part.astype(jnp.bfloat16),
        down_total[:, rank:].astype(jnp.bfloat16),
        up_v_part.astype(jnp.bfloat16),
    )


def solution(mesh):
    return jax.shard_map(
        per_device,
        mesh=mesh,
        in_specs=(
            P(("blk", "uly"), None),
            P(("blk", "uly"), None),
            P(("blk", "uly"), None),
            P(("blk", "uly"), None),
            P(("blk", "uly"), None),
            P(),
            P(),
            P(),
            P(),
        ),
        out_specs=(P(("blk", "uly"), None), P(), P(None, "uly"), P(), P(None, "uly")),
        check_vma=False,
    )
```

profile of v0, /device:TPU:0, one launch (start us, length us, event | category | flops | bytes accessed | tf_op | source)
XLA Modules:
  0.0 393.2 jit_solution(3088520763562678787)
XLA Ops:
  8.0 1.3 copy-done
  9.3 1.7 convolution_convert_fusion.3
  12.7 4.2 %all-to-all-start.2 = ((bf16[128,2,2560]{2,0,1:T(8,128)(2,1)}), bf16[128,2,2560]{2,0,1:T(8,128)(2,1)S(1)}, u32[]{:S(2)}, u32[]{:S(2)}) async-start(bf16[128,2,2560]{2,0,1:T(8,128)(2,1)} %bitcast.73), calls=%async_computation.2 | async-start | bytes 2621440 | tf_op jit(solution)/shard_map/all_to_all | solution.py:52
  16.9 2.5 copy.47
  19.4 14.8 %all-to-all-done.2 = bf16[128,2,2560]{2,0,1:T(8,128)(2,1)S(1)} async-done(((bf16[128,2,2560]{2,0,1:T(8,128)(2,1)}), bf16[128,2,2560]{2,0,1:T(8,128)(2,1)S(1)}, u32[]{:S(2)}, u32[]{:S(2)}) %all-to-all-start.2) | async-done | bytes 1310752 | tf_op jit(solution)/shard_map/all_to_all | solution.py:52
  34.2 19.7 %all_to_all.95 = bf16[128,2,2560]{2,0,1:T(8,128)(2,1)S(1)} all-to-all(bf16[128,2,2560]{2,0,1:T(8,128)(2,1)} %bitcast.74), channel_id=1, replica_groups=mesh['blk'=16,'uly'=2] {'uly'}, dimensions={1} | all-to-all | bytes 2621440 | tf_op jit(solution)/shard_map/all_to_all | solution.py:51
  53.9 1.9 pad_maximum_fusion
  55.8 2.8 collective-permute-start
  58.6 2.5 copy.30
  61.1 4.6 %all-to-all-start.3 = ((bf16[128,2,2560]{0,2,1:T(8,128)(2,1)}), bf16[128,2,2560]{0,2,1:T(8,128)(2,1)}, u32[]{:S(2)}, u32[]{:S(2)}) async-start(bf16[128,2,2560]{0,2,1:T(8,128)(2,1)} %bitcast.71), calls=%async_computation.3 | async-start | bytes 2621440 | tf_op jit(solution)/shard_map/all_to_all | solution.py:53
  69.0 14.5 %all-to-all-done.3 = bf16[128,2,2560]{0,2,1:T(8,128)(2,1)} async-done(((bf16[128,2,2560]{0,2,1:T(8,128)(2,1)}), bf16[128,2,2560]{0,2,1:T(8,128)(2,1)}, u32[]{:S(2)}, u32[]{:S(2)}) %all-to-all-start.3) | async-done | bytes 1310752 | tf_op jit(solution)/shard_map/all_to_all | solution.py:53
  83.4 4.5 %all-to-all-start = ((bf16[128,2,2560]{2,0,1:T(8,128)(2,1)}), bf16[128,2,2560]{2,0,1:T(8,128)(2,1)}, u32[]{:S(2)}, u32[]{:S(2)}) async-start(bf16[128,2,2560]{2,0,1:T(8,128)(2,1)} %bitcast.70), calls=%async_computation | async-start | bytes 2621440 | tf_op jit(solution)/shard_map/all_to_all | solution.py:50
  88.0 2.5 copy.31
  90.4 2.0 slice_bitcast_fusion
  92.5 2.5 pad_maximum_fusion.1
  95.1 9.7 %all-to-all-done = bf16[128,2,2560]{2,0,1:T(8,128)(2,1)} async-done(((bf16[128,2,2560]{2,0,1:T(8,128)(2,1)}), bf16[128,2,2560]{2,0,1:T(8,128)(2,1)}, u32[]{:S(2)}, u32[]{:S(2)}) %all-to-all-start) | async-done | bytes 1310752 | tf_op jit(solution)/shard_map/all_to_all | solution.py:50
  104.8 1.8 broadcast_in_dim.43
  106.5 1.9 broadcast_in_dim.43.clone
  109.6 139.5 %while.20 = (s32[]{:T(128)}, bf16[256,2560]{1,0:T(8,128)(2,1)}, bf16[256,2560]{1,0:T(8,128)(2,1)S(1)}, f32[256,2560]{1,0:T(8,128)}, f32[256,2560]{1,0:T(8,128)},...) while((s32[]{:T(128)}, bf16[256,2560]{1,0:T(8,128)(2,1)}, ...), condition=%wide.region_4.5_spmd.clone, body=%wide.region_0.4_spmd.clone.sunk | while | flops 169574656 | bytes 4862660 | solution.py:84
  109.7 1.3 fusion.70
  114.5 1.4 fusion.71
  116.6 1.3 fusion.70
  121.5 1.4 fusion.71
  123.6 1.3 fusion.70
  128.4 1.4 fusion.71
  135.4 1.4 fusion.71
  137.5 1.3 fusion.70
  142.3 1.4 fusion.71
  144.5 1.3 fusion.70
  149.4 1.4 fusion.71
  151.5 1.3 fusion.70
  156.3 1.4 fusion.71
  158.5 1.3 fusion.70
  163.3 1.4 fusion.71
  170.3 1.4 fusion.71
  172.4 1.3 fusion.70
  177.3 1.4 fusion.71
  179.4 1.3 fusion.70
  184.3 1.4 fusion.71
  191.2 1.4 fusion.71
  193.3 1.3 fusion.70
  198.2 1.4 fusion.71
  205.2 1.4 fusion.71
  212.1 1.4 fusion.71
  214.3 1.3 fusion.70
  219.1 1.4 fusion.71
  226.1 1.4 fusion.71
  228.2 1.3 fusion.70
  233.0 1.4 fusion.71
  240.1 1.4 fusion.71
  242.2 1.3 fusion.70
  247.0 1.4 fusion.71
  249.2 1.3 collective-permute-start.1
  250.5 4.7 %all-to-all-start.4 = ((bf16[2,128,2560]{2,1,0:T(8,128)(2,1)}), bf16[2,128,2560]{2,1,0:T(8,128)(2,1)}, u32[]{:S(2)}, u32[]{:S(2)}) async-start(bf16[2,128,2560]{2,1,0:T(8,128)(2,1)} %bitcast.72), calls=%async_computation.4 | async-start | bytes 2621440 | tf_op jit(solution)/shard_map/all_to_all | solution.py:91
  255.2 18.3 %all_gather.3 = bf16[256,128]{0,1:T(8,128)(2,1)S(1)} all-gather(bf16[128,128]{0,1:T(8,128)(2,1)S(1)} %pad_maximum_fusion.4), channel_id=1, replica_groups=mesh['blk'=16,'uly'=2] {'uly'}, dimensions={0}, use_global_device_ids=true | all-gather | bytes 98304 | tf_op jit(solution)/shard_map/all_gather | solution.py:92
  275.1 1.8 copy.35
  276.9 1.4 copy.36
  278.3 2.9 add_convert_fusion
  283.6 12.9 %reduce-scatter.2.cloned.1.call-done = f32[128,128]{0,1:T(8,128)} async-done(((f32[256,128]{0,1:T(8,128)}), f32[128,128]{0,1:T(8,128)}) %reduce-scatter.2.cloned.1.call-update) | async-done | bytes 65552 | tf_op jit(solution)/shard_map/reduce_scatter | solution.py:102
  296.4 2.8 convolution_bitcast_fusion
  299.3 74.1 %all-reduce.5 = bf16[5120,128]{0,1:T(8,128)(2,1)S(1)} all-reduce(f32[5120,128]{0,1:T(8,128)} %convolution_bitcast_fusion), channel_id=1, replica_groups=mesh['blk'=16,'uly'=2] {'blk','uly'}, use_global_device_ids=true, to_apply=%region_6.7 | all-reduce | flops 655360 | bytes 3932160 | tf_op jit(solution)/shard_map/psum | solution.py:105
  374.5 7.9 %all-reduce.4.cloned.1.call-done = (bf16[64,2560]{1,0:T(8,128)(2,1)}, bf16[64,2560]{1,0:T(8,128)(2,1)}) async-done(((bf16[64,2560]{1,0:T(8,128)(2,1)}, bf16[64,2560]{1,0:T(8,128)(2,1)}), (bf16[64,2560]{1,0:T(8,128)(2,1)}, bf16[64,2560]{1,0:T(8,128)(2,1)})) %all-reduce.4.cloned.1.call-update) | async-done | bytes 655376 | tf_op jit(solution)/shard_map/psum | solution.py:109
  382.4 1.7 copy.76
  384.1 1.7 copy.77
  (267 shorter events, 106.5 us)
Async XLA Ops:
  8.0 1.3 copy-start
  8.0 3.0 copy-start.7
  8.0 3.0 copy-start.5
  12.7 21.5 %all-to-all-start.2 = ((bf16[128,2,2560]{2,0,1:T(8,128)(2,1)}), bf16[128,2,2560]{2,0,1:T(8,128)(2,1)S(1)}, u32[]{:S(2)}, u32[]{:S(2)}) async-start(bf16[128,2,2560]{2,0,1:T(8,128)(2,1)} %bitcast.73), calls=%async_computation.2 | async-start | bytes 2621440 | tf_op jit(solution)/shard_map/all_to_all | solution.py:52
  53.9 1.9 copy-start.1
  55.8 34.6 %collective-permute-start = (bf16[2,256,2560]{2,1,0:T(8,128)(2,1)}, bf16[2,256,2560]{2,1,0:T(8,128)(2,1)}, u32[]{:S(2)}, u32[]{:S(2)}) collective-permute-start(bf16[2,256,2560]{2,1,0:T(8,128)(2,1)} %pad_maximum_fusion), channel_id=1, source_target_pairs={{0,2},{2,4},{4,6},{6,8},{8,10},{10,12},{12,14},{14,16},{16,18},{18... | collective-permute-start | bytes 7864328 | tf_op jit(solution)/shard_map/ppermute | solution.py:12
  61.1 4.7 %copy-start.9 = (bf16[5120,64]{0,1:T(8,128)(2,1)S(1)}, bf16[5120,64]{0,1:T(8,128)(2,1)}, u32[]{:S(2)}) copy-start(bf16[5120,64]{0,1:T(8,128)(2,1)} %param.16) | copy-start | bytes 1966084
  61.1 22.3 %all-to-all-start.3 = ((bf16[128,2,2560]{0,2,1:T(8,128)(2,1)}), bf16[128,2,2560]{0,2,1:T(8,128)(2,1)}, u32[]{:S(2)}, u32[]{:S(2)}) async-start(bf16[128,2,2560]{0,2,1:T(8,128)(2,1)} %bitcast.71), calls=%async_computation.3 | async-start | bytes 2621440 | tf_op jit(solution)/shard_map/all_to_all | solution.py:53
  65.8 1.1 copy-start.3
  65.8 1.5 copy-start.8
  83.4 21.3 %all-to-all-start = ((bf16[128,2,2560]{2,0,1:T(8,128)(2,1)}), bf16[128,2,2560]{2,0,1:T(8,128)(2,1)}, u32[]{:S(2)}, u32[]{:S(2)}) async-start(bf16[128,2,2560]{2,0,1:T(8,128)(2,1)} %bitcast.70), calls=%async_computation | async-start | bytes 2621440 | tf_op jit(solution)/shard_map/all_to_all | solution.py:50
  90.4 2.1 copy-start.2
  249.2 29.1 %collective-permute-start.1 = (f32[256,2560]{1,0:T(8,128)}, f32[256,2560]{1,0:T(8,128)}, u32[]{:S(2)}, u32[]{:S(2)}) collective-permute-start(f32[256,2560]{1,0:T(8,128)} %get-tuple-element.180), channel_id=1, source_target_pairs={{2,0},{4,2},{6,4},{8,6},{10,8},{12,10},{14,12},{16,14},{18,16},{20... | collective-permute-start | bytes 7864328 | tf_op jit(solution)/shard_map/ppermute | solution.py:12
  250.4 23.0 %copy-start.4 = (bf16[64,5120]{1,0:T(8,128)(2,1)S(1)}, bf16[64,5120]{1,0:T(8,128)(2,1)}, u32[]{:S(2)}) copy-start(bf16[64,5120]{1,0:T(8,128)(2,1)} %param.17) | copy-start | bytes 1966084
  250.5 24.6 %all-to-all-start.4 = ((bf16[2,128,2560]{2,1,0:T(8,128)(2,1)}), bf16[2,128,2560]{2,1,0:T(8,128)(2,1)}, u32[]{:S(2)}, u32[]{:S(2)}) async-start(bf16[2,128,2560]{2,1,0:T(8,128)(2,1)} %bitcast.72), calls=%async_computation.4 | async-start | bytes 2621440 | tf_op jit(solution)/shard_map/all_to_all | solution.py:91
  255.1 41.3 %reduce-scatter.2.cloned.1.call-start = ((), (), s32[]{:S(2)}) async-start(), calls=%async_computation.6 | async-start | bytes 196608 | tf_op jit(solution)/shard_map/reduce_scatter | solution.py:102
  278.3 2.9 copy-start.6
  282.4 99.9 %all-reduce.4.cloned.1.call-start = ((), (), s32[]{:S(2)}) async-start(), calls=%async_computation.7 | async-start | bytes 1310720 | tf_op jit(solution)/shard_map/psum | solution.py:109
Sparse Core Ops, SparseCore 0:
  282.5 13.8 reduce-scatter.1
Sparse Core Ops, SparseCore 1:
  286.9 95.4 all-reduce.3
where the time goes:
time: 396 us; the launch traced here: 393 us
  blocking collectives  112 us (28%)
  matrix products  89.7 us (23%)
  local copies, waits for them, and re-layouts  76.7 us (19%)
  waiting for transfers between devices  59.7 us (15%)
  starting transfers between devices  22.2 us (6%)
  other arithmetic  16.2 us (4%)
  between operations  15.7 us (4%)
    psum x1, blocking collectives, per_device(): down_total = lax.psum(inner(tokens, lowrank), ('blk', 'uly'))  74.1 us
    dot_general x20, matrix products, head_pass(): jnp.dot(score_grad, keys, preferred_element_type=jnp.float32) * scale  27.2 us
    dot_general x20, matrix products, head_pass(): scores = jnp.dot(query, keys.T, preferred_element_type=jnp.float32) * scale  25.1 us
    dot_general x20, matrix products, head_pass(): jnp.dot(probs, values, preferred_element_type=jnp.float32)  23.1 us
    all_to_all x1, blocking collectives, per_device(): lax.all_to_all(key_base, 'uly', split_axis=1, concat_axis=0, tiled=True)  19.7 us
    dynamic_slice x40, local copies, waits for them, and re-layouts, per_head(): lax.dynamic_slice_in_dim(upstream_h, start, HEAD, 1)  19.1 us
    all_gather x1, blocking collectives, per_device(): lax.all_gather(jnp.concatenate([low_q, low_v], 1), 'uly', axis=0, tiled=T...  18.3 us
    dynamic_update_slice x20, local copies, waits for them, and re-layouts, per_head(): lax.dynamic_update_slice_in_dim(prior_terms, result[2][:rows], start, 1)  15.6 us
  transfers between devices with their start and end apart: 8, of which 5 were waited for; matrix products, arithmetic and copies ran while one was open for 6% of the time, Pallas kernels for 0%

commit v1 on v0

--- a/solution.py
+++ b/solution.py
@@ -102,7 +102,10 @@
     lowrank = lax.psum_scatter(partial_rank, "uly", scatter_dimension=0, tiled=True).astype(
         jnp.bfloat16
     )
-    down_total = lax.psum(inner(tokens, lowrank), ("blk", "uly"))
+    write_sheet = lambda base_x, a_name, axis_tag: lax.psum(
+        lax.psum(base_x, axis_name=a_name), axis_name=axis_tag
+    )
+    down_total = write_sheet(inner(tokens, lowrank), "uly", "blk")
     up_q_terms = inner(block_lows[:, :rank], query_grad_h)
     up_v_terms = inner(block_lows[:, rank:], value_grad_h)
     up_q_part, up_v_part = (

time: 396 us -> 501 us (1.27)
  waiting for transfers between devices: 59.7 us -> 145 us
  blocking collectives: 112 us -> 129 us
    psum x0 -> x1, waiting for transfers between devices: none -> 44.8 us  [per_device(): lax.psum(base_x, axis_name=a_name)]
    reduce_scatter x1, waiting for transfers between devices: 12.9 us -> 36 us  [per_device(): lax.psum_scatter(partial_rank, 'uly', scatter_dimension=0, tiled=True)]
    all_gather x1, blocking collectives: 18.3 us -> 32.1 us  [per_device(): lax.all_gather(jnp.concatenate([low_q, low_v], 1), 'uly', axis=0, tiled=T...]
    psum x1, waiting for transfers between devices: 7.86 us -> 21.1 us  [per_device(): lax.psum(up_q_terms.astype(jnp.bfloat16), 'blk').astype(jnp.float32)]
    unnamed x24 -> x26, local copies, waits for them, and re-layouts: 9.74 us -> 11.9 us
  transfers between devices with their start and end apart: 8 -> 9, of which waited for: 5 -> 7; matrix products, arithmetic and copies ran while one was open for 6% -> 5% of each run, Pallas kernels for 0% -> 0%
where the time goes in v1:
time: 501 us; the launch traced here: 498 us
  waiting for transfers between devices  145 us (29%)
  blocking collectives  129 us (26%)
  matrix products  90.7 us (18%)
  local copies, waits for them, and re-layouts  79.7 us (16%)
  starting transfers between devices  22.1 us (4%)
  other arithmetic  16.2 us (3%)
  between operations  13.9 us (3%)
    psum x1, blocking collectives, per_device(): lax.psum(lax.psum(base_x, axis_name=a_name), axis_name=axis_tag)  77.1 us
    psum x1, waiting for transfers between devices, per_device(): lax.psum(base_x, axis_name=a_name)  44.8 us
    reduce_scatter x1, waiting for transfers between devices, per_device(): lax.psum_scatter(partial_rank, 'uly', scatter_dimension=0, tiled=True)  36 us
    all_gather x1, blocking collectives, per_device(): lax.all_gather(jnp.concatenate([low_q, low_v], 1), 'uly', axis=0, tiled=T...  32.1 us
    dot_general x20, matrix products, head_pass(): jnp.dot(score_grad, keys, preferred_element_type=jnp.float32) * scale  27.2 us
    dot_general x20, matrix products, head_pass(): scores = jnp.dot(query, keys.T, preferred_element_type=jnp.float32) * scale  25.1 us
    dot_general x20, matrix products, head_pass(): jnp.dot(probs, values, preferred_element_type=jnp.float32)  23.1 us
    psum x1, waiting for transfers between devices, per_device(): lax.psum(up_q_terms.astype(jnp.bfloat16), 'blk').astype(jnp.float32)  21.1 us
  transfers between devices with their start and end apart: 9, of which 7 were waited for; matrix products, arithmetic and copies ran while one was open for 5% of the time, Pallas kernels for 0%

profile of v1, /device:TPU:0, one launch (start us, length us, event | category | flops | bytes accessed | tf_op | source)
XLA Modules:
  0.0 497.6 jit_solution(5049458562276672925)
XLA Ops:
  7.2 1.3 copy-done
  8.5 1.7 convolution_convert_fusion.3
  11.9 4.2 all-to-all-start.2
  16.1 2.5 copy.47
  18.6 14.8 %all-to-all-done.2 = bf16[128,2,2560]{2,0,1:T(8,128)(2,1)S(1)} async-done(((bf16[128,2,2560]{2,0,1:T(8,128)(2,1)}), bf16[128,2,2560]{2,0,1:T(8,128)(2,1)S(1)}, u32[]{:S(2)}, u32[]{:S(2)}) %all-to-all-start.2) | async-done | bytes 1310752 | tf_op jit(solution)/shard_map/all_to_all | solution.py:52
  33.4 19.7 %all_to_all.95 = bf16[128,2,2560]{2,0,1:T(8,128)(2,1)S(1)} all-to-all(bf16[128,2,2560]{2,0,1:T(8,128)(2,1)} %bitcast.74), channel_id=1, replica_groups=mesh['blk'=16,'uly'=2] {'uly'}, dimensions={1} | all-to-all | bytes 2621440 | tf_op jit(solution)/shard_map/all_to_all | solution.py:51
  53.1 1.9 pad_maximum_fusion
  55.0 2.8 collective-permute-start
  57.9 2.5 copy.30
  60.4 4.6 all-to-all-start.3
  68.2 14.4 %all-to-all-done.3 = bf16[128,2,2560]{0,2,1:T(8,128)(2,1)} async-done(((bf16[128,2,2560]{0,2,1:T(8,128)(2,1)}), bf16[128,2,2560]{0,2,1:T(8,128)(2,1)}, u32[]{:S(2)}, u32[]{:S(2)}) %all-to-all-start.3) | async-done | bytes 1310752 | tf_op jit(solution)/shard_map/all_to_all | solution.py:53
  82.6 4.5 all-to-all-start
  87.2 2.5 copy.31
  89.7 2.0 slice_bitcast_fusion
  91.8 2.5 pad_maximum_fusion.1
  94.3 9.6 %all-to-all-done = bf16[128,2,2560]{2,0,1:T(8,128)(2,1)} async-done(((bf16[128,2,2560]{2,0,1:T(8,128)(2,1)}), bf16[128,2,2560]{2,0,1:T(8,128)(2,1)}, u32[]{:S(2)}, u32[]{:S(2)}) %all-to-all-start) | async-done | bytes 1310752 | tf_op jit(solution)/shard_map/all_to_all | solution.py:50
  103.9 1.8 broadcast_in_dim.43
  105.7 1.9 broadcast_in_dim.43.clone
  108.8 139.5 %while.20 = (s32[]{:T(128)}, bf16[256,2560]{1,0:T(8,128)(2,1)}, bf16[256,2560]{1,0:T(8,128)(2,1)S(1)}, f32[256,2560]{1,0:T(8,128)}, f32[256,2560]{1,0:T(8,128)},...) while((s32[]{:T(128)}, bf16[256,2560]{1,0:T(8,128)(2,1)}, ...), condition=%wide.region_4.5_spmd.clone, body=%wide.region_0.4_spmd.clone.sunk | while | flops 169574656 | bytes 4862660 | solution.py:84
  108.8 1.3 fusion.70
  113.7 1.4 fusion.71
  115.8 1.3 fusion.70
  120.7 1.4 fusion.71
  127.7 1.4 fusion.71
  134.7 1.4 fusion.71
  141.7 1.4 fusion.71
  143.8 1.3 fusion.70
  148.6 1.4 fusion.71
  150.8 1.3 fusion.70
  155.6 1.4 fusion.71
  157.7 1.3 fusion.70
  162.6 1.4 fusion.71
  164.7 1.3 fusion.70
  169.5 1.4 fusion.71
  176.5 1.4 fusion.71
  183.5 1.4 fusion.71
  190.5 1.4 fusion.71
  192.6 1.3 fusion.70
  197.4 1.4 fusion.71
  204.4 1.4 fusion.71
  211.4 1.4 fusion.71
  213.6 1.3 fusion.70
  218.4 1.4 fusion.71
  225.3 1.4 fusion.71
  232.3 1.4 fusion.71
  234.4 1.3 fusion.70
  239.3 1.4 fusion.71
  241.4 1.3 fusion.70
  246.2 1.4 fusion.71
  248.3 1.3 collective-permute-start.1
  249.6 1.5 fusion.26
  251.1 4.3 collective-permute-done.1
  255.5 2.9 add_convert_fusion
  260.7 36.0 %reduce-scatter.2.cloned.1.call-done = f32[128,128]{0,1:T(8,128)} async-done(((f32[256,128]{0,1:T(8,128)}), f32[128,128]{0,1:T(8,128)}) %reduce-scatter.2.cloned.1.call-update) | async-done | bytes 65552 | tf_op jit(solution)/shard_map/reduce_scatter | solution.py:102
  296.8 2.8 convolution_bitcast_fusion
  299.6 4.5 all-to-all-start.4
  304.2 32.1 %all_gather.3 = bf16[256,128]{0,1:T(8,128)(2,1)S(1)} all-gather(bf16[128,128]{0,1:T(8,128)(2,1)S(1)} %pad_maximum_fusion.4), channel_id=1, replica_groups=mesh['blk'=16,'uly'=2] {'uly'}, dimensions={0}, use_global_device_ids=true | all-gather | bytes 98304 | tf_op jit(solution)/shard_map/all_gather | solution.py:92
  337.4 2.5 copy.35
  340.0 2.5 copy.36
  343.6 44.8 %all-reduce.5.cloned.1.call-done = f32[5120,128]{0,1:T(8,128)} async-done(((f32[5120,128]{0,1:T(8,128)}), f32[5120,128]{0,1:T(8,128)}) %all-reduce.5.cloned.1.call-update) | async-done | bytes 2621456 | tf_op jit(solution)/shard_map/psum | solution.py:106
  388.3 77.1 %all-reduce.8 = bf16[5120,128]{0,1:T(8,128)(2,1)S(1)} all-reduce(f32[5120,128]{0,1:T(8,128)} %all-reduce.5.cloned.1.call-done), channel_id=1, replica_groups=mesh['blk'=16,'uly'=2] {'blk'}, use_global_device_ids=true, to_apply=%region_7.8 | all-reduce | flops 655360 | bytes 3932160 | tf_op jit(solution)/shard_map/psum | solution.py:105
  466.6 21.1 %all-reduce.7.cloned.1.call-done = (bf16[64,2560]{1,0:T(8,128)(2,1)}, bf16[64,2560]{1,0:T(8,128)(2,1)}) async-done(((bf16[64,2560]{1,0:T(8,128)(2,1)}, bf16[64,2560]{1,0:T(8,128)(2,1)}), (bf16[64,2560]{1,0:T(8,128)(2,1)}, bf16[64,2560]{1,0:T(8,128)(2,1)})) %all-reduce.7.cloned.1.call-update) | async-done | bytes 655376 | tf_op jit(solution)/shard_map/psum | solution.py:112
  487.7 1.7 copy.77
  489.4 1.7 copy.78
  (272 shorter events, 110.9 us)
Async XLA Ops:
  7.2 1.3 copy-start
  7.2 3.0 copy-start.8
  7.2 3.0 copy-start.6
  11.9 21.5 %all-to-all-start.2 = ((bf16[128,2,2560]{2,0,1:T(8,128)(2,1)}), bf16[128,2,2560]{2,0,1:T(8,128)(2,1)S(1)}, u32[]{:S(2)}, u32[]{:S(2)}) async-start(bf16[128,2,2560]{2,0,1:T(8,128)(2,1)} %bitcast.73), calls=%async_computation.2 | async-start | bytes 2621440 | tf_op jit(solution)/shard_map/all_to_all | solution.py:52
  53.1 1.9 copy-start.1
  55.0 34.6 %collective-permute-start = (bf16[2,256,2560]{2,1,0:T(8,128)(2,1)}, bf16[2,256,2560]{2,1,0:T(8,128)(2,1)}, u32[]{:S(2)}, u32[]{:S(2)}) collective-permute-start(bf16[2,256,2560]{2,1,0:T(8,128)(2,1)} %pad_maximum_fusion), channel_id=1, source_target_pairs={{0,2},{2,4},{4,6},{6,8},{8,10},{10,12},{12,14},{14,16},{16,18},{18... | collective-permute-start | bytes 7864328 | tf_op jit(solution)/shard_map/ppermute | solution.py:12
  60.4 4.7 copy-start.10
  60.4 22.3 %all-to-all-start.3 = ((bf16[128,2,2560]{0,2,1:T(8,128)(2,1)}), bf16[128,2,2560]{0,2,1:T(8,128)(2,1)}, u32[]{:S(2)}, u32[]{:S(2)}) async-start(bf16[128,2,2560]{0,2,1:T(8,128)(2,1)} %bitcast.71), calls=%async_computation.3 | async-start | bytes 2621440 | tf_op jit(solution)/shard_map/all_to_all | solution.py:53
  65.0 1.1 copy-start.5
  65.0 1.5 copy-start.9
  82.6 21.3 %all-to-all-start = ((bf16[128,2,2560]{2,0,1:T(8,128)(2,1)}), bf16[128,2,2560]{2,0,1:T(8,128)(2,1)}, u32[]{:S(2)}, u32[]{:S(2)}) async-start(bf16[128,2,2560]{2,0,1:T(8,128)(2,1)} %bitcast.70), calls=%async_computation | async-start | bytes 2621440 | tf_op jit(solution)/shard_map/all_to_all | solution.py:50
  87.2 209.6 %reduce-scatter.2.cloned.1.call-start = ((), (), s32[]{:S(2)}) async-start(), calls=%async_computation.6 | async-start | bytes 196608 | tf_op jit(solution)/shard_map/reduce_scatter | solution.py:102
  89.7 2.1 copy-start.2
  248.3 7.1 %collective-permute-start.1 = (f32[256,2560]{1,0:T(8,128)}, f32[256,2560]{1,0:T(8,128)}, u32[]{:S(2)}, u32[]{:S(2)}) collective-permute-start(f32[256,2560]{1,0:T(8,128)} %get-tuple-element.180), channel_id=1, source_target_pairs={{2,0},{4,2},{6,4},{8,6},{10,8},{12,10},{14,12},{16,14},{18,16},{20... | collective-permute-start | bytes 7864328 | tf_op jit(solution)/shard_map/ppermute | solution.py:12
  255.5 4.0 copy-start.7
  258.4 1.1 copy-start.3
  260.7 127.7 %all-reduce.5.cloned.1.call-start = ((), (), s32[]{:S(2)}) async-start(), calls=%async_computation.7 | async-start | bytes 5242880 | tf_op jit(solution)/shard_map/psum | solution.py:106
  299.6 37.8 %all-to-all-start.4 = ((bf16[2,128,2560]{2,1,0:T(8,128)(2,1)}), bf16[2,128,2560]{2,1,0:T(8,128)(2,1)}, u32[]{:S(2)}, u32[]{:S(2)}) async-start(bf16[2,128,2560]{2,1,0:T(8,128)(2,1)} %bitcast.72), calls=%async_computation.4 | async-start | bytes 2621440 | tf_op jit(solution)/shard_map/all_to_all | solution.py:91
  304.2 183.5 %all-reduce.7.cloned.1.call-start = ((), (), s32[]{:S(2)}) async-start(), calls=%async_computation.8 | async-start | bytes 1310720 | tf_op jit(solution)/shard_map/psum | solution.py:112
  340.0 2.5 copy-start.4
Sparse Core Ops, SparseCore 0:
  260.8 35.9 reduce-scatter.1
  299.7 88.5 all-reduce.4
  392.4 95.2 all-reduce.6
